TPU v7x, 32 devices: a whole 2x2x4 slice. The times are simulated.
32 devices in a mesh: dp: 8 (over y, x, core), space: 4 (over z).
Axes of the slice: x: 2, y: 2, z: 4, core: 2. Of those that a mesh axis runs over, the one named last changes fastest.
Arguments:
- inputs: bfloat16 [64, 32, 32, 1024], P('dp', None, 'space'), may hold values from 0 to 2
- conv_in: bfloat16 [64, 864], replicated, may hold values from -0.21875 to 0.21875
- norm_gain: float32 [64], replicated, may hold values from 0.5 to 1.5
- norm_shift: float32 [64], replicated, may hold values from -3 to 3
- conv_out: bfloat16 [128, 1728], replicated, may hold values from -0.15625 to 0.15625
- dense_in: bfloat16 [65536, 128], replicated, may hold values from -0.0234375 to 0.0234375
- dense_out: bfloat16 [128, 4], replicated, may hold values from -0.5 to 0.5
- targets: float32 [64, 4], P(('dp', 'space')), may hold values from -6 to 6
Outputs:
- grad_conv_in: float32 [64, 864], replicated
- grad_norm: float32 [2, 64], replicated
- grad_conv_out: float32 [128, 1728], replicated
- grad_dense_in: float32 [65536, 128], P(('dp', 'space'))
- grad_dense_out: float32 [128, 4], replicated
- predictions: float32 [64, 4], P(('dp', 'space'))
All inputs are finite; a program needn't handle non-finite values.
Results may differ from a plain program's by a relative error of at most 0.015.
Values may be sent and summed in bfloat16 or wider, within the bound.
No kernel may reach another device: no remote copies, remote signals or barrier semaphores. Data moves between devices by JAX's collectives and lax.ppermute only.
A program may use at most 256 MiB of HBM per device.

v0:
```python
import jax
import jax.numpy as jnp
from jax import lax
from jax.sharding import PartitionSpec as P

C_OUT = 128
GRID = 32
norm_epsilon = 1e-05


def extended_2(cells, sides, width):
    for axis, dim in sides:
        count = lax.axis_size(axis)
        ends = count - 1
        head = lax.slice_in_dim(cells, 0, width, axis=dim)
        tail = lax.slice_in_dim(cells, cells.shape[dim] - width, cells.shape[dim], axis=dim)
        cells = jnp.concatenate(
            [
                lax.ppermute(tail, axis, [(i, (i + 1) % count) for i in range(ends)]),
                cells,
                lax.ppermute(head, axis, [((i + 1) % count, i) for i in range(ends)]),
            ],
            axis=dim,
        )
    return cells


def leaky_relu(values):
    return 0.65 * values + 0.35 * values * jnp.tanh(values)


def slope_of(values):
    bent = jnp.tanh(values)
    return 0.65 + 0.35 * (bent + values * (1.0 - bent * bent))


def plane_shift(volume, step_y, step_z, extent):
    plane_len = extent * extent
    offset = step_y * extent + step_z
    margin = extent + 1
    pad_widths = [(0, 0)] * (volume.ndim - 1) + [(margin, margin)]
    padded = jnp.pad(volume, pad_widths)
    shifted = lax.slice_in_dim(
        padded, margin + offset, margin + offset + plane_len, axis=volume.ndim - 1
    )
    column = lax.broadcasted_iota(jnp.int32, (plane_len,), 0) % extent
    inside = ((column + step_z >= 0) & (column + step_z < extent)).astype(volume.dtype)
    return shifted * inside


def columns(slab_ext, planes, extent):
    pieces = []
    for step_x in (-1, 0, 1):
        plane_set = lax.slice_in_dim(slab_ext, 1 + step_x, 1 + step_x + planes, axis=1)
        for step_y in (-1, 0, 1):
            for step_z in (-1, 0, 1):
                pieces.append(plane_shift(plane_set, step_y, step_z, extent))
    stacked = jnp.stack(pieces, 0)
    return stacked.reshape(len(pieces) * slab_ext.shape[0], planes * extent * extent)


def pad_planes(volume, extent):
    shaped = volume.reshape(volume.shape[0], extent, extent * extent)
    return jnp.pad(shaped, ((0, 0), (1, 1), (0, 0)))


def pool_slab(active, planes, extent):
    samples, channels = (active.shape[0], active.shape[1])
    blocks = active.reshape(samples, channels, planes // 2, 2, extent // 2, 2, extent // 2, 2)
    return (blocks.sum(axis=(3, 5, 7)) * 0.125).reshape(samples, channels, -1)


def unpool_slab(gradient, planes, extent):
    samples, channels = (gradient.shape[0], gradient.shape[1])
    blocks = gradient.reshape(samples, channels, planes // 2, 1, extent // 2, 1, extent // 2, 1)
    wide = jnp.broadcast_to(
        blocks, (samples, channels, planes // 2, 2, extent // 2, 2, extent // 2, 2)
    )
    return wide.reshape(samples, channels, planes * extent * extent) * 0.125


def shards(inputs, conv_in, norm_gain, norm_shift, conv_out, dense_in, dense_out, targets):
    half_grid = GRID // 2
    quarter = GRID // 4
    cell_count = inputs.shape[0] * GRID**3
    extended = extended_2(inputs, (("space", 2),), 1)
    planes = extended.shape[2] - 2

    def first_conv(slab_ext):
        return jnp.dot(conv_in, columns(slab_ext, planes, GRID), preferred_element_type=jnp.float32)

    first_out = lax.map(first_conv, extended)
    local_sum = jnp.sum(first_out, axis=(0, 2))
    average = lax.psum(local_sum, "space") / cell_count
    centred = first_out - average[None, :, None]
    variance = lax.psum(jnp.sum(centred * centred, axis=(0, 2)), "space") / cell_count
    inverse = lax.rsqrt(variance + norm_epsilon)
    whitened = centred * inverse[None, :, None]
    normed = norm_gain[None, :, None] * whitened + norm_shift[None, :, None]
    pooled = pool_slab(leaky_relu(normed), planes, GRID).astype(jnp.bfloat16)
    samples_pooled = lax.all_to_all(pooled, "space", split_axis=0, concat_axis=2, tiled=True)

    def second_conv(volume):
        return jnp.dot(
            conv_out,
            columns(pad_planes(volume, half_grid), half_grid, half_grid),
            preferred_element_type=jnp.float32,
        )

    second_out = lax.map(second_conv, samples_pooled)
    local_samples = second_out.shape[0]
    features = (
        pool_slab(leaky_relu(second_out), half_grid, half_grid)
        .reshape(local_samples, -1)
        .astype(jnp.bfloat16)
    )
    hidden_pre = jnp.dot(features, dense_in, preferred_element_type=jnp.float32)
    hidden = leaky_relu(hidden_pre).astype(jnp.bfloat16)
    predictions = jnp.dot(hidden, dense_out, preferred_element_type=jnp.float32)
    misfit = predictions - targets
    grad_out_local = jnp.dot(hidden.astype(jnp.float32).T, misfit, precision=lax.Precision.HIGHEST)
    back_hidden = (
        jnp.dot(misfit, dense_out.astype(jnp.float32).T, precision=lax.Precision.HIGHEST)
        * slope_of(hidden_pre)
    ).astype(jnp.bfloat16)
    partial_rows = lax.psum_scatter(
        lax.dot_general(
            features, back_hidden, (((0,), (0,)), ((), ())), preferred_element_type=jnp.float32
        ).astype(jnp.bfloat16),
        "dp",
        scatter_dimension=0,
        tiled=True,
    )
    grad_dense_in = lax.psum_scatter(partial_rows, "space", scatter_dimension=0, tiled=True).astype(
        jnp.float32
    )
    back_features = lax.dot_general(
        back_hidden, dense_in, (((1,), (1,)), ((), ())), preferred_element_type=jnp.float32
    )
    back_features = back_features.reshape(local_samples, C_OUT, quarter**3)
    back_second = (unpool_slab(back_features, half_grid, half_grid) * slope_of(second_out)).astype(
        jnp.bfloat16
    )

    def second_back(running, couple):
        volume, gradient = couple
        padded = pad_planes(volume, half_grid)
        patches = columns(padded, half_grid, half_grid)
        running = running + lax.dot_general(
            gradient, patches, (((1,), (1,)), ((), ())), preferred_element_type=jnp.float32
        )
        patch_grad = lax.dot_general(
            conv_out, gradient, (((0,), (0,)), ((), ())), preferred_element_type=jnp.float32
        )
        _, unfold = jax.vjp(
            lambda whole_pad: columns(whole_pad, half_grid, half_grid), padded.astype(jnp.float32)
        )
        volume_grad = unfold(patch_grad)[0][:, 1:-1, :]
        return (running, volume_grad.reshape(volume.shape).astype(jnp.bfloat16))

    grad_conv_out, back_pooled = lax.scan(
        second_back, jnp.zeros(conv_out.shape, jnp.float32), (samples_pooled, back_second)
    )
    back_slab = lax.all_to_all(back_pooled, "space", split_axis=2, concat_axis=0, tiled=True)
    back_active = unpool_slab(back_slab.astype(jnp.float32), planes, GRID) * slope_of(normed)
    sum_grad = jnp.sum(back_active, axis=(0, 2))
    sum_xgrad = jnp.sum(back_active * whitened, axis=(0, 2))
    group_grad, group_xgrad = lax.psum((sum_grad, sum_xgrad), "space")
    back_first = (norm_gain * inverse)[None, :, None] * (
        back_active
        - group_grad[None, :, None] / cell_count
        - whitened * group_xgrad[None, :, None] / cell_count
    )
    back_first = back_first.astype(jnp.bfloat16)

    def first_back(running, couple):
        slab_ext, gradient = couple
        patches = columns(slab_ext, planes, GRID)
        return (
            running
            + lax.dot_general(
                gradient, patches, (((1,), (1,)), ((), ())), preferred_element_type=jnp.float32
            ),
            None,
        )

    grad_conv_in, _ = lax.scan(
        first_back, jnp.zeros(conv_in.shape, jnp.float32), (extended, back_first)
    )
    grad_norm_local = jnp.stack([sum_xgrad, sum_grad])
    summed = lax.psum(
        (grad_conv_in, grad_norm_local, grad_conv_out, grad_out_local), ("dp", "space")
    )
    return (summed[0], summed[1], summed[2], grad_dense_in, summed[3], predictions)


def solution(mesh):
    placed = (P("dp", None, "space", None), P(), P(), P(), P(), P(), P(), P(("dp", "space"), None))
    return jax.shard_map(
        shards,
        mesh=mesh,
        in_specs=placed,
        out_specs=(P(), P(), P(), P(("dp", "space"), None), P(), P(("dp", "space"), None)),
        check_vma=False,
    )
```

profile of v0, /device:TPU:0, one launch (start us, length us, event | category | flops | bytes accessed | tf_op | source)
XLA Modules:
  0.0 1239.6 jit_solution(6425463289631794915)
XLA Ops:
  20.0 9.6 collective-permute-done
  34.9 9.2 pad_maximum_fusion
  44.1 170.7 %while.52 = (s32[]{:T(128)}, f32[8,64,8192]{2,1,0:T(8,128)}, bf16[8,32,10,1024]{3,2,1,0:T(8,128)(2,1)}, bf16[64,864]{1,0:T(8,128)(2,1)S(1)}, s32[]{:T(128)}) while((s32[]{:T(128)}, f32[8,64,8192]{2,1,0:T(8,128)}, bf16[8,32,10,1024]{3,2,1,0:T(8,128)(2,1)}, bf16[64,864]{1,0:T(8,128)(2,1)S(1)}, s32[]{:T(128)}) %tuple.218), condition=%wide.region_1.2_spmd, body=%wide.region_0.1_spmd.sunk | while | flops 934313984 | bytes 77505088 | solution.py:92
  52.5 8.8 copy.138
  73.8 8.8 copy.138
  95.2 8.8 copy.138
  116.5 8.8 copy.138
  137.8 8.8 copy.138
  159.2 8.8 copy.138
  180.5 8.8 copy.138
  201.9 8.8 copy.138
  214.8 23.5 %copy.52 = f32[8,64,8192]{1,0,2:T(8,128)} copy(f32[8,64,8192]{2,1,0:T(8,128)} %get-tuple-element.251) | data formatting | bytes 33554432 | tf_op jit(solution)/shard_map/while | solution.py:92
  238.3 6.9 reduce_sum.54
  245.2 9.9 psum.56
  255.2 15.0 %multiply_reduce_fusion.1 = f32[64]{0:T(128)S(1)} fusion(f32[8,64,8192]{1,0,2:T(8,128)} %copy.52, f32[64]{0:T(128)S(1)} %broadcast_multiply_fusion.1), kind=kLoop, calls=%fused_computation.417 | loop fusion | flops 12582848 | bytes 16777728 | tf_op jit(solution)/shard_map/reduce_sum | solution.py:96
  270.2 9.0 psum.57
  279.8 25.5 %fusion.222 = f32[8,64,8192]{1,0,2:T(8,128)} fusion(f32[8,64,8192]{1,0,2:T(8,128)} %copy.52, f32[64]{0:T(128)S(1)} %copy-done.23, f32[64]{0:T(128)S(1)} %get-tuple-element.447, f32[64]{0:T(128)S(1)} %copy-done.19, f32[64]{0:T(128)S(1)} %broadcast_multiply_fusion.1), kind=kLoop, calls=%fused_computation.415 | loop fusion | flops 33554432 | bytes 33555456 | tf_op jit(solution)/shard_map/add | solution.py:29
  305.3 14.9 %reduce_sum.56 = f32[8,64,4,16,16]{1,0,4,3,2:T(8,128)} reduce(f32[8,64,4,2,16,2,16,2]{1,0,7,6,5,4,3,2:T(8,128)} %bitcast.865, f32[]{:T(128)} %constant.649.clone.1), dimensions={3,5,7}, to_apply=%region_6.7 | reduce | flops 3670016 | bytes 18874372 | tf_op jit(solution)/shard_map/reduce_sum | solution.py:70
  331.2 21.0 %all-to-all-done = bf16[8,64,1024]{2,1,0:T(8,128)(2,1)S(1)} async-done(((bf16[8,64,1024]{2,1,0:T(8,128)(2,1)}), bf16[8,64,1024]{2,1,0:T(8,128)(2,1)S(1)}, u32[]{:S(2)}, u32[]{:S(2)}) %all-to-all-start) | async-done | bytes 1048608 | tf_op jit(solution)/shard_map/all_to_all | solution.py:101
  352.4 35.7 %while.53 = (s32[]{:T(128)}, f32[2,128,4096]{1,2,0:T(8,128)}, bf16[2,64,4096]{2,1,0:T(8,128)(2,1)S(1)}, bf16[128,1728]{0,1:T(8,128)(2,1)S(1)}, s32[]{:T(128)}) while((s32[]{:T(128)}, f32[2,128,4096]{1,2,0:T(8,128)}, bf16[2,64,4096]{2,1,0:T(8,128)(2,1)S(1)}, bf16[128,1728]{0,1:T(8,128)(2,1)S(1)}, s32[]{:T(128)}) %tuple.217), condition=%wide.region_8.9_spmd, body=%wide.region_7.8_spmd.sunk | while | flops 1840259072 | bytes 77004352 | solution.py:110
  404.7 6.8 convert_element_type.690
  411.5 7.3 fusion.227
  419.6 10.2 convolution_multiply_fusion
  429.8 9.3 convolution_convert_fusion
  439.2 8.1 mul.1737
  458.9 268.3 %while.54 = (s32[]{:T(128)}, f32[128,1728]{0,1:T(8,128)}, bf16[2,64,4096]{2,1,0:T(8,128)(2,1)}, bf16[2,128,4096]{1,2,0:T(8,128)(2,1)S(1)}, bf16[2,64,4096]{2,1,0...) while((s32[]{:T(128)}, f32[128,1728]{0,1:T(8,128)}, ...), condition=%wide.region_11.12_spmd.clone, body=%wide.region_10.11_spmd.clone.sunk | while | flops 3666803200 | bytes 362422176 | solution.py:161
  481.5 12.6 %convolution_bitcast_fusion.4 = f32[1728,4096]{1,0:T(8,128)} fusion(bf16[128,1728]{0,1:T(8,128)(2,1)} %get-tuple-element.749, bf16[2,128,4096]{1,2,0:T(8,128)(2,1)S(1)} %get-tuple-element.747, s32[]{:T(128)} %get-tuple-element.736), kind=kOutput, calls=%fused_computation.158.clone.1 | convolution fusion | flops 1811939328 | bytes 29802500 | tf_op jit(solution)/shard_map/while/body/eval_jaxpr/dot_general | solution.py:152
  494.1 10.4 fusion.376
  523.3 7.2 bitcast_multiply_fusion.35
  556.2 7.2 fusion.379
  565.2 8.3 fusion.380
  582.9 9.4 copy.169
  592.3 8.2 convolution_add_fusion.4
  602.1 12.2 convolution_bitcast_fusion.4
  614.3 9.8 fusion.376
  642.6 6.8 bitcast_multiply_fusion.35
  675.0 6.9 fusion.379
  683.8 8.1 fusion.380
  701.2 9.4 copy.169
  710.6 8.4 convolution_add_fusion.4
  738.6 23.6 %all-to-all-done.1 = bf16[4,2,65536]{2,1,0:T(2,128)(2,1)S(1)} async-done(((bf16[4,2,65536]{2,1,0:T(2,128)(2,1)}), bf16[4,2,65536]{2,1,0:T(2,128)(2,1)S(1)}, u32[]{:S(2)}, u32[]{:S(2)}) %all-to-all-start.1) | async-done | bytes 1048608 | tf_op jit(solution)/shard_map/all_to_all | solution.py:164
  778.5 22.3 %fusion.223 = (f32[64]{0:T(128)S(1)}, f32[64]{0:T(128)S(1)}) fusion(f32[8,64,8192]{1,0,2:T(8,128)} %copy.52, f32[8,64,4,16,16]{1,0,4,3,2:T(8,128)S(1)} %copy.62, f32[64]{0:T(128)S(1)} %copy-done.24, f32[64]{0:T(128)S(1)} %copy-done.22, f32[64]{0:T(128)S(1)} %copy-done.20, f32[64]{0:T(128)S(1)} %copy-done.18), kind=kLoop, calls=%fused_computation.419 | loop fusion | flops 58720128 | bytes 18875904 | tf_op jit(solution)/shard_map/reduce_sum | solution.py:166
  800.8 9.8 all-reduce.43
  810.6 25.9 %multiply_convert_fusion = bf16[8,64,8192]{1,0,2:T(8,128)(2,1)} fusion(f32[8,64,8192]{1,0,2:T(8,128)} %copy.52, f32[64]{0:T(128)S(1)} %get-tuple-element.374, f32[64]{0:T(128)S(1)} %broadcast_multiply_fusion, f32[8,64,4,16,16]{1,0,4,3,2:T(8,128)} %copy-done.11, f32[64]{0:T(128)S(1)} %copy-done.24, f32[64]{0:T(128)S(1)} %copy-done.22, f32[64]{0:T(128)S(1)} %copy-done.20, ...), kind=kLoop, calls=%fused_computation.412 | loop fusion | flops 71303168 | bytes 27264768 | tf_op jit(solution)/shard_map/convert_element_type | solution.py:174
  836.5 18.4 %copy.63 = bf16[8,64,8192]{2,1,0:T(8,128)(2,1)} copy(bf16[8,64,8192]{1,0,2:T(8,128)(2,1)} %multiply_convert_fusion) | data formatting | bytes 16777216
  855.0 242.5 %while.55 = (s32[]{:T(128)}, f32[64,864]{1,0:T(8,128)S(1)}, bf16[8,64,8192]{2,1,0:T(8,128)(2,1)}, bf16[8,32,10,1024]{3,2,1,0:T(8,128)(2,1)}, s32[]{:T(128)}, /*index=5*/s32[]{:T(128)}) while((s32[]{:T(128)}, f32[64,864]{1,0:T(8,128)S(1)}, bf16[8,64,8192]{2,1,0:T(8,128)(2,1)}, bf16[8,32,10,1024]{3,2,1,0:T(8,128)(2,1)}, ...), condition=%wide.region_17.18_spmd.clone, body=%wide.region_16.17_spmd.clone.sunk | while | flops 934424576 | bytes 76788304 | solution.py:187
  863.6 12.1 copy.170
  875.8 9.8 convolution_add_fusion.5
  894.0 12.1 copy.170
  906.2 9.7 convolution_add_fusion.5
  924.3 12.1 copy.170
  936.4 9.7 convolution_add_fusion.5
  954.6 12.1 copy.170
  966.7 9.7 convolution_add_fusion.5
  984.9 12.1 copy.170
  997.0 9.7 convolution_add_fusion.5
  1015.1 12.1 copy.170
  1027.3 9.7 convolution_add_fusion.5
  1045.4 12.1 copy.170
  1057.6 9.7 convolution_add_fusion.5
  1075.7 12.1 copy.170
  1087.8 9.7 convolution_add_fusion.5
  1098.5 39.9 %all-reduce.41 = (f32[2,64]{1,0:T(2,128)}, f32[128,4]{0,1:T(4,128)}) all-reduce(f32[2,64]{1,0:T(2,128)S(1)} %pad_maximum_fusion.1, f32[128,4]{0,1:T(4,128)S(1)} %fusion.228), channel_id=1, replica_groups=mesh['dp'=8,'space'=4] {'dp','space'}, use_global_device_ids=true, to_apply=%region_19.20 | all-reduce | flops 640 | bytes 5120 | tf_op jit(solution)/shard_map/psum | solution.py:191
  1140.5 87.6 %all-reduce.46.cloned.1.call-done = (f32[64,864]{1,0:T(8,128)}, f32[128,1728]{0,1:T(8,128)}) async-done(((f32[64,864]{1,0:T(8,128)}, f32[128,1728]{0,1:T(8,128)}), (f32[64,864]{1,0:T(8,128)}, f32[128,1728]{0,1:T(8,128)})) %all-reduce.46.cloned.1.call-update) | async-done | bytes 1105936 | tf_op jit(solution)/shard_map/psum | solution.py:191
  (861 shorter events, 404.5 us)
Async XLA Ops:
  8.0 410.8 %copy-start = (bf16[128,4]{0,1:T(4,128)(2,1)S(1)}, bf16[128,4]{0,1:T(4,128)(2,1)}, u32[]{:S(2)}) copy-start(bf16[128,4]{0,1:T(4,128)(2,1)} %param.22) | copy-start | bytes 3076
  8.0 36.1 %copy-start.16 = (bf16[64,864]{1,0:T(8,128)(2,1)S(1)}, bf16[64,864]{1,0:T(8,128)(2,1)}, u32[]{:S(2)}) copy-start(bf16[64,864]{1,0:T(8,128)(2,1)} %param.17) | copy-start | bytes 331780
  13.6 16.1 %collective-permute-start = (bf16[8,32,1,1024]{3,1,2,0:T(8,128)(2,1)S(1)}, bf16[8,32,1,1024]{3,1,2,0:T(8,128)(2,1)S(1)}, u32[]{:S(2)}, u32[]{:S(2)}) collective-permute-start(bf16[8,32,1,1024]{3,1,2,0:T(8,128)(2,1)S(1)} %copy.67), channel_id=1, source_target_pairs={{0,1},{1,2},{2,3},{4,5},{5,6},{6,7},{8,9},{9,10},{10,11},{12,13},{... | collective-permute-start | bytes 1572872 | tf_op jit(solution)/shard_map/ppermute | solution.py:19
  18.7 15.3 %collective-permute-start.1 = (bf16[8,32,1,1024]{3,1,2,0:T(8,128)(2,1)S(1)}, bf16[8,32,1,1024]{3,1,2,0:T(8,128)(2,1)S(1)}, u32[]{:S(2)}, u32[]{:S(2)}) collective-permute-start(bf16[8,32,1,1024]{3,1,2,0:T(8,128)(2,1)S(1)} %copy.68), channel_id=1, source_target_pairs={{1,0},{2,1},{3,2},{5,4},{6,5},{7,6},{9,8},{10,9},{11,10},{13,12},{... | collective-permute-start | bytes 1572872 | tf_op jit(solution)/shard_map/ppermute | solution.py:21
  255.2 24.6 %copy-start.17 = (f32[64]{0:T(128)}, f32[64]{0:T(128)S(1)}, u32[]{:S(2)}) copy-start(f32[64]{0:T(128)S(1)} %broadcast_multiply_fusion.1) | copy-start | bytes 772
  255.2 24.1 %copy-start.19 = (f32[64]{0:T(128)S(1)}, f32[64]{0:T(128)}, u32[]{:S(2)}) copy-start(f32[64]{0:T(128)} %param.18) | copy-start | bytes 772
  255.2 24.6 %copy-start.23 = (f32[64]{0:T(128)S(1)}, f32[64]{0:T(128)}, u32[]{:S(2)}) copy-start(f32[64]{0:T(128)} %param.19) | copy-start | bytes 772
  279.8 25.5 %copy-start.21 = (f32[64]{0:T(128)}, f32[64]{0:T(128)S(1)}, u32[]{:S(2)}) copy-start(f32[64]{0:T(128)S(1)} %get-tuple-element.447) | copy-start | bytes 772
  305.3 47.0 %copy-start.14 = (bf16[128,1728]{0,1:T(8,128)(2,1)S(1)}, bf16[128,1728]{0,1:T(8,128)(2,1)}, u32[]{:S(2)}) copy-start(bf16[128,1728]{0,1:T(8,128)(2,1)} %param.20) | copy-start | bytes 1327108
  327.6 24.6 %all-to-all-start = ((bf16[8,64,1024]{2,1,0:T(8,128)(2,1)}), bf16[8,64,1024]{2,1,0:T(8,128)(2,1)S(1)}, u32[]{:S(2)}, u32[]{:S(2)}) async-start(bf16[8,64,1024]{2,1,0:T(8,128)(2,1)} %copy.54), calls=%async_computation | async-start | bytes 2097152 | tf_op jit(solution)/shard_map/all_to_all | solution.py:101
  331.2 523.7 %reduce-scatter.3.cloned.1.call-start = ((), (), s32[]{:S(2)}) async-start(), calls=%async_computation.4 | async-start | bytes 18874368 | tf_op jit(solution)/shard_map/reduce_scatter | solution.py:126
  404.7 14.8 %copy-start.28 = (f32[2,4]{1,0:T(2,128)S(1)}, f32[2,4]{1,0:T(2,128)}, u32[]{:S(2)}) copy-start(f32[2,4]{1,0:T(2,128)} %param.23) | copy-start | bytes 100
  418.8 0.6 copy-start.26
  418.9 0.6 copy-start.30
  479.8 1.0 copy-start.9
  479.8 1.7 copy-start.12
  519.4 11.2 copy-start.4
  519.4 12.5 %copy-start.3 = (f32[64,4096]{1,0:T(8,128)S(1)}, f32[64,4096]{1,0:T(8,128)}, u32[]{:S(2)}) copy-start(f32[64,4096]{1,0:T(8,128)} %get-tuple-element.634) | copy-start | bytes 3145732 | tf_op jit(solution)/shard_map/while
  520.7 12.6 %copy-start.2 = (f32[64,4096]{1,0:T(8,128)S(1)}, f32[64,4096]{1,0:T(8,128)}, u32[]{:S(2)}) copy-start(f32[64,4096]{1,0:T(8,128)} %get-tuple-element.635) | copy-start | bytes 3145732 | tf_op jit(solution)/shard_map/while
  530.6 9.5 copy-start.6
  530.6 10.8 copy-start.5
  531.9 10.8 copy-start.7
  533.2 9.4 copy-start.8
  582.8 9.4 copy-start.13
  592.3 8.2 copy-start.10
  600.4 1.0 copy-start.9
  600.4 1.6 copy-start.12
  638.6 10.8 copy-start.4
  638.6 12.1 copy-start.3
  639.9 12.2 copy-start.2
  649.4 9.5 copy-start.6
  649.4 10.8 copy-start.5
  650.7 10.7 copy-start.7
  652.1 9.4 copy-start.8
  701.2 9.4 copy-start.13
  710.6 8.4 copy-start.10
  734.9 27.2 %all-to-all-start.1 = ((bf16[4,2,65536]{2,1,0:T(2,128)(2,1)}), bf16[4,2,65536]{2,1,0:T(2,128)(2,1)S(1)}, u32[]{:S(2)}, u32[]{:S(2)}) async-start(bf16[4,2,65536]{2,1,0:T(2,128)(2,1)} %reshape.317), calls=%async_computation.1 | async-start | bytes 2097152 | tf_op jit(solution)/shard_map/all_to_all | solution.py:164
  738.5 400.0 %reduce-scatter.5.cloned.1.call-start = ((), (), s32[]{:S(2)}) async-start(), calls=%async_computation.5 | async-start | bytes 2621440 | tf_op jit(solution)/shard_map/reduce_scatter | solution.py:134
  738.5 39.9 %copy-start.18 = (f32[64]{0:T(128)S(1)}, f32[64]{0:T(128)}, u32[]{:S(2)}) copy-start(f32[64]{0:T(128)} %copy-done.17) | copy-start | bytes 772
  738.5 39.9 %copy-start.20 = (f32[64]{0:T(128)S(1)}, f32[64]{0:T(128)}, u32[]{:S(2)}) copy-start(f32[64]{0:T(128)} %param.18) | copy-start | bytes 772
  738.5 39.9 %copy-start.22 = (f32[64]{0:T(128)S(1)}, f32[64]{0:T(128)}, u32[]{:S(2)}) copy-start(f32[64]{0:T(128)} %copy-done.21) | copy-start | bytes 772
  738.6 39.9 %copy-start.24 = (f32[64]{0:T(128)S(1)}, f32[64]{0:T(128)}, u32[]{:S(2)}) copy-start(f32[64]{0:T(128)} %param.19) | copy-start | bytes 772
  778.5 22.3 %copy-start.11 = (f32[8,64,4,16,16]{1,0,4,3,2:T(8,128)}, f32[8,64,4,16,16]{1,0,4,3,2:T(8,128)S(1)}, u32[]{:S(2)}) copy-start(f32[8,64,4,16,16]{1,0,4,3,2:T(8,128)S(1)} %copy.62) | copy-start | bytes 6291460
  778.5 32.2 %copy-start.25 = (f32[64]{0:T(128)S(1)}, f32[64]{0:T(128)}, u32[]{:S(2)}) copy-start(f32[64]{0:T(128)} %get-tuple-element.446) | copy-start | bytes 772
  854.9 373.2 %all-reduce.46.cloned.1.call-start = ((), (), s32[]{:S(2)}) async-start(), calls=%async_computation.6 | async-start | bytes 2228224 | tf_op jit(solution)/shard_map/psum | solution.py:191
  855.0 243.3 %copy-start.27 = (bf16[2,128]{1,0:T(2,128)(2,1)S(1)}, bf16[2,128]{1,0:T(2,128)(2,1)}, u32[]{:S(2)}) copy-start(bf16[2,128]{1,0:T(2,128)(2,1)} %copy-done.26) | copy-start | bytes 1540
  855.0 243.3 %copy-start.29 = (f32[2,4]{1,0:T(2,128)S(1)}, f32[2,4]{1,0:T(2,128)}, u32[]{:S(2)}) copy-start(f32[2,4]{1,0:T(2,128)} %param.23) | copy-start | bytes 100
  855.0 243.3 %copy-start.31 = (f32[2,4]{1,0:T(2,128)S(1)}, f32[2,4]{1,0:T(2,128)}, u32[]{:S(2)}) copy-start(f32[2,4]{1,0:T(2,128)} %copy-done.30) | copy-start | bytes 100
  1097.6 0.7 copy-start.15
  1097.6 134.3 %copy-start.1 = (bf16[128,4]{0,1:T(4,128)(2,1)S(1)}, bf16[128,4]{0,1:T(4,128)(2,1)}, u32[]{:S(2)}) copy-start(bf16[128,4]{0,1:T(4,128)(2,1)} %param.22) | copy-start | bytes 3076
Sparse Core Ops, SparseCore 0:
  459.0 115.2 reduce-scatter.2
  855.0 42.4 reduce-scatter.4
Sparse Core Ops, SparseCore 1:
  1098.4 129.7 all-reduce.45
where the time goes:
time: 1250 us; the launch traced here: 1240 us
  local copies, waits for them, and re-layouts  443 us (35%)
  other arithmetic  328 us (26%)
  matrix products  190 us (15%)
  waiting for transfers between devices  145 us (12%)
  blocking collectives  68.7 us (5%)
  loops' own time  34.6 us (3%)
  between operations  16.2 us (1%)
  starting transfers between devices  13.4 us (1%)
    while x122, local copies, waits for them, and re-layouts  269 us
    while x520, other arithmetic  123 us
    psum x1, waiting for transfers between devices, shards(): lax.psum((grad_conv_in, grad_norm_local, grad_conv_out, grad_out_local),...  87.6 us
    dot_general x8, matrix products, first_back(): lax.dot_general(gradient, patches, (((1,), (1,)), ((), ())), preferred_el...  77.7 us
    psum x1, blocking collectives, shards(): lax.psum((grad_conv_in, grad_norm_local, grad_conv_out, grad_out_local),...  39.9 us
    dot_general x8, matrix products, first_conv(): jnp.dot(conv_in, columns(slab_ext, planes, GRID), preferred_element_type=...  32.8 us
    another operation x4, local copies, waits for them, and re-layouts, columns(): stacked = jnp.stack(pieces, 0)  31.5 us
    add x2, other arithmetic, leaky_relu(): return 0.65 * values + 0.35 * values * jnp.tanh(values)  30.5 us
  transfers between devices with their start and end apart: 7, of which 5 were waited for; matrix products, arithmetic and copies ran while one was open for 46% of the time, Pallas kernels for 0%

commit v1 on v0

--- a/solution.py
+++ b/solution.py
@@ -189,7 +189,7 @@
     )
     grad_norm_local = jnp.stack([sum_xgrad, sum_grad])
     summed = lax.psum(
-        (grad_conv_in, grad_norm_local, grad_conv_out, grad_out_local), ("dp", "space")
+        lax.psum((grad_conv_in, grad_norm_local, grad_conv_out, grad_out_local), "space"), "dp"
     )
     return (summed[0], summed[1], summed[2], grad_dense_in, summed[3], predictions)
 

time: 1250 us -> 1220 us (0.976)
  blocking collectives: 68.7 us -> 43.4 us
    psum x1, waiting for transfers between devices: 87.6 us -> 52.7 us  [shards(): lax.psum((grad_conv_in, grad_norm_local, grad_conv_out, grad_out_local),...]
    reduce_scatter x1, waiting for transfers between devices: 0.01 us -> 30.7 us  [shards(): lax.psum_scatter(partial_rows, 'space', scatter_dimension=0, tiled=True)]
    psum x1, blocking collectives: 39.9 us -> 14.4 us  [shards(): lax.psum(lax.psum((grad_conv_in, grad_norm_local, grad_conv_out, grad_out...]
    all_to_all x1, waiting for transfers between devices: 23.6 us -> 10.9 us  [shards(): lax.all_to_all(back_pooled, 'space', split_axis=2, concat_axis=0, tiled=T...]
    unnamed x49 -> x55, local copies, waits for them, and re-layouts: 28 us -> 28.8 us
  transfers between devices with their start and end apart: 7 -> 8, of which waited for: 5 -> 7; matrix products, arithmetic and copies ran while one was open for 46% -> 28% of each run, Pallas kernels for 0% -> 0%
where the time goes in v1:
time: 1220 us; the launch traced here: 1210 us
  local copies, waits for them, and re-layouts  444 us (36%)
  other arithmetic  328 us (27%)
  matrix products  192 us (16%)
  waiting for transfers between devices  138 us (11%)
  blocking collectives  43.4 us (4%)
  loops' own time  34.4 us (3%)
  between operations  16.1 us (1%)
  starting transfers between devices  13.5 us (1%)
    while x122, local copies, waits for them, and re-layouts  269 us
    while x520, other arithmetic  123 us
    dot_general x8, matrix products, first_back(): lax.dot_general(gradient, patches, (((1,), (1,)), ((), ())), preferred_el...  77.6 us
    psum x1, waiting for transfers between devices, shards(): lax.psum((grad_conv_in, grad_norm_local, grad_conv_out, grad_out_local),...  52.7 us
    dot_general x8, matrix products, first_conv(): jnp.dot(conv_in, columns(slab_ext, planes, GRID), preferred_element_type=...  32.8 us
    reduce_scatter x1, waiting for transfers between devices, shards(): lax.psum_scatter(partial_rows, 'space', scatter_dimension=0, tiled=True)  30.7 us
    another operation x4, local copies, waits for them, and re-layouts, columns(): stacked = jnp.stack(pieces, 0)  30.5 us
    add x2, other arithmetic, leaky_relu(): return 0.65 * values + 0.35 * values * jnp.tanh(values)  30.5 us
  transfers between devices with their start and end apart: 8, of which 7 were waited for; matrix products, arithmetic and copies ran while one was open for 28% of the time, Pallas kernels for 0%

profile of v1, /device:TPU:0, one launch (start us, length us, event | category | flops | bytes accessed | tf_op | source)
XLA Modules:
  0.0 1208.9 jit_solution(4057913297306282948)
XLA Ops:
  20.0 9.6 collective-permute-done
  34.8 9.2 pad_maximum_fusion
  44.0 170.8 %while.52 = (s32[]{:T(128)}, f32[8,64,8192]{2,1,0:T(8,128)}, bf16[8,32,10,1024]{3,2,1,0:T(8,128)(2,1)}, bf16[64,864]{1,0:T(8,128)(2,1)S(1)}, s32[]{:T(128)}) while((s32[]{:T(128)}, f32[8,64,8192]{2,1,0:T(8,128)}, bf16[8,32,10,1024]{3,2,1,0:T(8,128)(2,1)}, bf16[64,864]{1,0:T(8,128)(2,1)S(1)}, s32[]{:T(128)}) %tuple.221), condition=%wide.region_1.2_spmd, body=%wide.region_0.1_spmd.sunk | while | flops 934313984 | bytes 77505088 | solution.py:92
  52.5 8.8 copy.138
  73.8 8.8 copy.138
  95.1 8.8 copy.138
  116.4 8.8 copy.138
  137.8 8.8 copy.138
  159.2 8.8 copy.138
  180.5 8.8 copy.138
  201.9 8.8 copy.138
  214.8 23.5 %copy.52 = f32[8,64,8192]{1,0,2:T(8,128)} copy(f32[8,64,8192]{2,1,0:T(8,128)} %get-tuple-element.251) | data formatting | bytes 33554432 | tf_op jit(solution)/shard_map/while | solution.py:92
  238.3 6.9 reduce_sum.54
  245.2 9.9 psum.84
  255.1 15.0 %multiply_reduce_fusion.1 = f32[64]{0:T(128)S(1)} fusion(f32[8,64,8192]{1,0,2:T(8,128)} %copy.52, f32[64]{0:T(128)S(1)} %broadcast_multiply_fusion.1), kind=kLoop, calls=%fused_computation.417 | loop fusion | flops 12582848 | bytes 16777728 | tf_op jit(solution)/shard_map/reduce_sum | solution.py:96
  270.2 9.0 psum.85
  279.7 25.6 %fusion.222 = f32[8,64,8192]{1,0,2:T(8,128)} fusion(f32[8,64,8192]{1,0,2:T(8,128)} %copy.52, f32[64]{0:T(128)S(1)} %copy-done.24, f32[64]{0:T(128)S(1)} %get-tuple-element.451, f32[64]{0:T(128)S(1)} %copy-done.20, f32[64]{0:T(128)S(1)} %broadcast_multiply_fusion.1), kind=kLoop, calls=%fused_computation.415 | loop fusion | flops 33554432 | bytes 33555456 | tf_op jit(solution)/shard_map/add | solution.py:29
  305.3 15.0 %reduce_sum.56 = f32[8,64,4,16,16]{1,0,4,3,2:T(8,128)} reduce(f32[8,64,4,2,16,2,16,2]{1,0,7,6,5,4,3,2:T(8,128)} %bitcast.865, f32[]{:T(128)} %constant.649.clone.1), dimensions={3,5,7}, to_apply=%region_6.7 | reduce | flops 3670016 | bytes 18874372 | tf_op jit(solution)/shard_map/reduce_sum | solution.py:70
  331.2 21.1 %all-to-all-done = bf16[8,64,1024]{2,1,0:T(8,128)(2,1)S(1)} async-done(((bf16[8,64,1024]{2,1,0:T(8,128)(2,1)}), bf16[8,64,1024]{2,1,0:T(8,128)(2,1)S(1)}, u32[]{:S(2)}, u32[]{:S(2)}) %all-to-all-start) | async-done | bytes 1048608 | tf_op jit(solution)/shard_map/all_to_all | solution.py:101
  352.4 35.7 %while.53 = (s32[]{:T(128)}, f32[2,128,4096]{1,2,0:T(8,128)}, bf16[2,64,4096]{2,1,0:T(8,128)(2,1)S(1)}, bf16[128,1728]{0,1:T(8,128)(2,1)S(1)}, s32[]{:T(128)}) while((s32[]{:T(128)}, f32[2,128,4096]{1,2,0:T(8,128)}, bf16[2,64,4096]{2,1,0:T(8,128)(2,1)S(1)}, bf16[128,1728]{0,1:T(8,128)(2,1)S(1)}, s32[]{:T(128)}) %tuple.220), condition=%wide.region_8.9_spmd, body=%wide.region_7.8_spmd.sunk | while | flops 1840259072 | bytes 77004352 | solution.py:110
  411.5 7.4 fusion.227
  419.8 10.2 convolution_multiply_fusion
  430.0 8.1 mul.1737
  449.7 266.0 %while.54 = (s32[]{:T(128)}, f32[128,1728]{0,1:T(8,128)}, bf16[2,64,4096]{2,1,0:T(8,128)(2,1)}, bf16[2,128,4096]{1,2,0:T(8,128)(2,1)S(1)}, bf16[2,64,4096]{2,1,0...) while((s32[]{:T(128)}, f32[128,1728]{0,1:T(8,128)}, ...), condition=%wide.region_11.12_spmd.clone, body=%wide.region_10.11_spmd.clone.sunk | while | flops 3666803200 | bytes 362422176 | solution.py:161
  472.3 12.2 %convolution_bitcast_fusion.4 = f32[1728,4096]{1,0:T(8,128)} fusion(bf16[128,1728]{0,1:T(8,128)(2,1)} %get-tuple-element.753, bf16[2,128,4096]{1,2,0:T(8,128)(2,1)S(1)} %get-tuple-element.751, s32[]{:T(128)} %get-tuple-element.740), kind=kOutput, calls=%fused_computation.158.clone.1 | convolution fusion | flops 1811939328 | bytes 29802500 | tf_op jit(solution)/shard_map/while/body/eval_jaxpr/dot_general | solution.py:152
  484.6 9.7 fusion.376
  512.9 6.8 bitcast_multiply_fusion.35
  545.2 6.9 fusion.379
  553.9 8.1 fusion.380
  571.3 9.4 copy.169
  580.8 8.1 convolution_add_fusion.4
  590.6 12.2 %convolution_bitcast_fusion.4 = f32[1728,4096]{1,0:T(8,128)} fusion(bf16[128,1728]{0,1:T(8,128)(2,1)} %get-tuple-element.753, bf16[2,128,4096]{1,2,0:T(8,128)(2,1)S(1)} %get-tuple-element.751, s32[]{:T(128)} %get-tuple-element.740), kind=kOutput, calls=%fused_computation.158.clone.1 | convolution fusion | flops 1811939328 | bytes 29802500 | tf_op jit(solution)/shard_map/while/body/eval_jaxpr/dot_general | solution.py:152
  602.9 9.7 fusion.376
  663.5 6.9 fusion.379
  672.2 8.1 fusion.380
  689.6 9.4 copy.169
  699.1 8.4 convolution_add_fusion.4
  727.0 10.8 convolution_convert_fusion
  738.7 10.9 all-to-all-done.1
  767.0 22.5 %fusion.223 = (f32[64]{0:T(128)S(1)}, f32[64]{0:T(128)S(1)}) fusion(f32[8,64,8192]{1,0,2:T(8,128)} %copy.52, f32[8,64,4,16,16]{1,0,4,3,2:T(8,128)S(1)} %copy.62, f32[64]{0:T(128)S(1)} %copy-done.25, f32[64]{0:T(128)S(1)} %copy-done.23, f32[64]{0:T(128)S(1)} %copy-done.21, f32[64]{0:T(128)S(1)} %copy-done.19), kind=kLoop, calls=%fused_computation.419 | loop fusion | flops 58720128 | bytes 18875904 | tf_op jit(solution)/shard_map/reduce_sum | solution.py:166
  789.6 10.1 all-reduce.43
  799.6 26.1 %multiply_convert_fusion = bf16[8,64,8192]{1,0,2:T(8,128)(2,1)} fusion(f32[8,64,8192]{1,0,2:T(8,128)} %copy.52, f32[64]{0:T(128)S(1)} %get-tuple-element.374, f32[64]{0:T(128)S(1)} %broadcast_multiply_fusion, f32[8,64,4,16,16]{1,0,4,3,2:T(8,128)} %copy-done.11, f32[64]{0:T(128)S(1)} %copy-done.25, f32[64]{0:T(128)S(1)} %copy-done.23, f32[64]{0:T(128)S(1)} %copy-done.21, ...), kind=kLoop, calls=%fused_computation.412 | loop fusion | flops 71303168 | bytes 27264768 | tf_op jit(solution)/shard_map/convert_element_type | solution.py:174
  825.7 18.6 %copy.63 = bf16[8,64,8192]{2,1,0:T(8,128)(2,1)} copy(bf16[8,64,8192]{1,0,2:T(8,128)(2,1)} %multiply_convert_fusion) | data formatting | bytes 16777216
  844.3 242.4 %while.55 = (s32[]{:T(128)}, f32[64,864]{1,0:T(8,128)S(1)}, bf16[8,64,8192]{2,1,0:T(8,128)(2,1)}, bf16[8,32,10,1024]{3,2,1,0:T(8,128)(2,1)}, s32[]{:T(128)}, /*index=5*/s32[]{:T(128)}) while((s32[]{:T(128)}, f32[64,864]{1,0:T(8,128)S(1)}, bf16[8,64,8192]{2,1,0:T(8,128)(2,1)}, bf16[8,32,10,1024]{3,2,1,0:T(8,128)(2,1)}, ...), condition=%wide.region_17.18_spmd.clone, body=%wide.region_16.17_spmd.clone.sunk | while | flops 934424576 | bytes 76788304 | solution.py:187
  852.8 12.2 %copy.170 = bf16[108,8,8,1024]{3,1,2,0:T(8,128)(2,1)} copy(bf16[108,8,8,1024]{3,2,1,0:T(8,128)(2,1)S(1)} %bitcast.862) | data formatting | bytes 28311552 | tf_op jit(solution)/shard_map/while
  865.0 9.7 convolution_add_fusion.5
  883.1 12.2 %copy.170 = bf16[108,8,8,1024]{3,1,2,0:T(8,128)(2,1)} copy(bf16[108,8,8,1024]{3,2,1,0:T(8,128)(2,1)S(1)} %bitcast.862) | data formatting | bytes 28311552 | tf_op jit(solution)/shard_map/while
  895.3 9.7 convolution_add_fusion.5
  913.4 12.2 %copy.170 = bf16[108,8,8,1024]{3,1,2,0:T(8,128)(2,1)} copy(bf16[108,8,8,1024]{3,2,1,0:T(8,128)(2,1)S(1)} %bitcast.862) | data formatting | bytes 28311552 | tf_op jit(solution)/shard_map/while
  925.6 9.7 convolution_add_fusion.5
  943.7 12.2 %copy.170 = bf16[108,8,8,1024]{3,1,2,0:T(8,128)(2,1)} copy(bf16[108,8,8,1024]{3,2,1,0:T(8,128)(2,1)S(1)} %bitcast.862) | data formatting | bytes 28311552 | tf_op jit(solution)/shard_map/while
  955.9 9.7 convolution_add_fusion.5
  974.0 12.2 %copy.170 = bf16[108,8,8,1024]{3,1,2,0:T(8,128)(2,1)} copy(bf16[108,8,8,1024]{3,2,1,0:T(8,128)(2,1)S(1)} %bitcast.862) | data formatting | bytes 28311552 | tf_op jit(solution)/shard_map/while
  986.2 9.7 convolution_add_fusion.5
  1004.3 12.2 %copy.170 = bf16[108,8,8,1024]{3,1,2,0:T(8,128)(2,1)} copy(bf16[108,8,8,1024]{3,2,1,0:T(8,128)(2,1)S(1)} %bitcast.862) | data formatting | bytes 28311552 | tf_op jit(solution)/shard_map/while
  1016.4 9.7 convolution_add_fusion.5
  1034.6 12.2 %copy.170 = bf16[108,8,8,1024]{3,1,2,0:T(8,128)(2,1)} copy(bf16[108,8,8,1024]{3,2,1,0:T(8,128)(2,1)S(1)} %bitcast.862) | data formatting | bytes 28311552 | tf_op jit(solution)/shard_map/while
  1046.7 9.7 convolution_add_fusion.5
  1064.9 12.2 %copy.170 = bf16[108,8,8,1024]{3,1,2,0:T(8,128)(2,1)} copy(bf16[108,8,8,1024]{3,2,1,0:T(8,128)(2,1)S(1)} %bitcast.862) | data formatting | bytes 28311552 | tf_op jit(solution)/shard_map/while
  1077.0 9.7 convolution_add_fusion.5
  1088.1 52.7 %all-reduce.50.cloned.1.call-done = (f32[64,864]{1,0:T(8,128)}, f32[128,1728]{0,1:T(8,128)}) async-done(((f32[64,864]{1,0:T(8,128)}, f32[128,1728]{0,1:T(8,128)}), (f32[64,864]{1,0:T(8,128)}, f32[128,1728]{0,1:T(8,128)})) %all-reduce.50.cloned.1.call-update) | async-done | bytes 1105936 | tf_op jit(solution)/shard_map/psum | solution.py:192
  1140.8 14.4 %all-reduce.41 = (f32[2,64]{1,0:T(2,128)}, f32[128,4]{0,1:T(4,128)}) all-reduce(f32[2,64]{1,0:T(2,128)S(1)} %get-tuple-element.376, f32[128,4]{0,1:T(4,128)S(1)} %get-tuple-element.377), channel_id=1, replica_groups=mesh['dp'=8,'space'=4] {'dp'}, use_global_device_ids=true, to_apply=%region_21.22 | all-reduce | flops 640 | bytes 5120 | tf_op jit(solution)/shard_map/psum | solution.py:191
  1155.2 30.7 %reduce-scatter.5.cloned.1.call-done = bf16[2048,128]{1,0:T(8,128)(2,1)} async-done(((bf16[8192,128]{1,0:T(8,128)(2,1)}), bf16[2048,128]{1,0:T(8,128)(2,1)}) %reduce-scatter.5.cloned.1.call-update) | async-done | bytes 524304 | tf_op jit(solution)/shard_map/reduce_scatter | solution.py:134
  1188.0 9.4 all-reduce.48.cloned.1.call-done
  (870 shorter events, 420.0 us)
Async XLA Ops:
  8.0 411.0 %copy-start = (bf16[128,4]{0,1:T(4,128)(2,1)S(1)}, bf16[128,4]{0,1:T(4,128)(2,1)}, u32[]{:S(2)}) copy-start(bf16[128,4]{0,1:T(4,128)(2,1)} %param.22) | copy-start | bytes 3076
  8.0 36.0 %copy-start.17 = (bf16[64,864]{1,0:T(8,128)(2,1)S(1)}, bf16[64,864]{1,0:T(8,128)(2,1)}, u32[]{:S(2)}) copy-start(bf16[64,864]{1,0:T(8,128)(2,1)} %param.17) | copy-start | bytes 331780
  13.5 16.1 %collective-permute-start = (bf16[8,32,1,1024]{3,1,2,0:T(8,128)(2,1)S(1)}, bf16[8,32,1,1024]{3,1,2,0:T(8,128)(2,1)S(1)}, u32[]{:S(2)}, u32[]{:S(2)}) collective-permute-start(bf16[8,32,1,1024]{3,1,2,0:T(8,128)(2,1)S(1)} %copy.67), channel_id=1, source_target_pairs={{0,1},{1,2},{2,3},{4,5},{5,6},{6,7},{8,9},{9,10},{10,11},{12,13},{... | collective-permute-start | bytes 1572872 | tf_op jit(solution)/shard_map/ppermute | solution.py:19
  18.7 15.3 %collective-permute-start.1 = (bf16[8,32,1,1024]{3,1,2,0:T(8,128)(2,1)S(1)}, bf16[8,32,1,1024]{3,1,2,0:T(8,128)(2,1)S(1)}, u32[]{:S(2)}, u32[]{:S(2)}) collective-permute-start(bf16[8,32,1,1024]{3,1,2,0:T(8,128)(2,1)S(1)} %copy.68), channel_id=1, source_target_pairs={{1,0},{2,1},{3,2},{5,4},{6,5},{7,6},{9,8},{10,9},{11,10},{13,12},{... | collective-permute-start | bytes 1572872 | tf_op jit(solution)/shard_map/ppermute | solution.py:21
  255.1 24.6 %copy-start.18 = (f32[64]{0:T(128)}, f32[64]{0:T(128)S(1)}, u32[]{:S(2)}) copy-start(f32[64]{0:T(128)S(1)} %broadcast_multiply_fusion.1) | copy-start | bytes 772
  255.1 24.1 %copy-start.20 = (f32[64]{0:T(128)S(1)}, f32[64]{0:T(128)}, u32[]{:S(2)}) copy-start(f32[64]{0:T(128)} %param.18) | copy-start | bytes 772
  255.1 24.6 %copy-start.24 = (f32[64]{0:T(128)S(1)}, f32[64]{0:T(128)}, u32[]{:S(2)}) copy-start(f32[64]{0:T(128)} %param.19) | copy-start | bytes 772
  279.7 25.6 %copy-start.22 = (f32[64]{0:T(128)}, f32[64]{0:T(128)S(1)}, u32[]{:S(2)}) copy-start(f32[64]{0:T(128)S(1)} %get-tuple-element.451) | copy-start | bytes 772
  305.3 47.1 %copy-start.14 = (bf16[128,1728]{0,1:T(8,128)(2,1)S(1)}, bf16[128,1728]{0,1:T(8,128)(2,1)}, u32[]{:S(2)}) copy-start(bf16[128,1728]{0,1:T(8,128)(2,1)} %param.20) | copy-start | bytes 1327108
  327.7 24.6 %all-to-all-start = ((bf16[8,64,1024]{2,1,0:T(8,128)(2,1)}), bf16[8,64,1024]{2,1,0:T(8,128)(2,1)S(1)}, u32[]{:S(2)}, u32[]{:S(2)}) async-start(bf16[8,64,1024]{2,1,0:T(8,128)(2,1)} %copy.54), calls=%async_computation | async-start | bytes 2097152 | tf_op jit(solution)/shard_map/all_to_all | solution.py:101
  404.8 14.9 %copy-start.31 = (f32[2,4]{1,0:T(2,128)S(1)}, f32[2,4]{1,0:T(2,128)}, u32[]{:S(2)}) copy-start(f32[2,4]{1,0:T(2,128)} %param.23) | copy-start | bytes 100
  411.5 18.5 %copy-start.16 = (bf16[2,65536]{1,0:T(2,128)(2,1)}, bf16[2,65536]{1,0:T(2,128)(2,1)S(1)}, u32[]{:S(2)}) copy-start(bf16[2,65536]{1,0:T(2,128)(2,1)S(1)} %convert_element_type.690) | copy-start | bytes 786436
  419.0 0.5 copy-start.29
  419.1 0.6 copy-start.33
  419.8 18.3 %copy-start.26 = (bf16[2,128]{1,0:T(2,128)(2,1)}, bf16[2,128]{1,0:T(2,128)(2,1)S(1)}, u32[]{:S(2)}) copy-start(bf16[2,128]{1,0:T(2,128)(2,1)S(1)} %fusion.225) | copy-start | bytes 1540
  449.7 277.3 %copy-start.27 = (bf16[2,128]{1,0:T(2,128)(2,1)S(1)}, bf16[2,128]{1,0:T(2,128)(2,1)}, u32[]{:S(2)}) copy-start(bf16[2,128]{1,0:T(2,128)(2,1)} %copy-done.26) | copy-start | bytes 1540
  470.6 1.0 copy-start.9
  470.6 1.7 copy-start.12
  508.9 10.8 copy-start.4
  508.9 12.1 %copy-start.3 = (f32[64,4096]{1,0:T(8,128)S(1)}, f32[64,4096]{1,0:T(8,128)}, u32[]{:S(2)}) copy-start(f32[64,4096]{1,0:T(8,128)} %get-tuple-element.638) | copy-start | bytes 3145732 | tf_op jit(solution)/shard_map/while
  510.2 12.1 copy-start.2
  519.7 9.4 copy-start.6
  519.7 10.7 copy-start.5
  521.0 10.7 copy-start.7
  522.3 9.4 copy-start.8
  571.3 9.5 copy-start.13
  580.8 8.2 copy-start.10
  588.9 1.0 copy-start.9
  588.9 1.7 copy-start.12
  627.2 10.8 copy-start.4
  627.2 12.1 %copy-start.3 = (f32[64,4096]{1,0:T(8,128)S(1)}, f32[64,4096]{1,0:T(8,128)}, u32[]{:S(2)}) copy-start(f32[64,4096]{1,0:T(8,128)} %get-tuple-element.638) | copy-start | bytes 3145732 | tf_op jit(solution)/shard_map/while
  628.5 12.1 copy-start.2
  638.0 9.4 copy-start.6
  638.0 10.7 copy-start.5
  639.3 10.7 copy-start.7
  640.6 9.4 copy-start.8
  689.6 9.5 copy-start.13
  699.1 8.4 copy-start.10
  723.4 26.3 %all-to-all-start.1 = ((bf16[4,2,65536]{2,1,0:T(2,128)(2,1)}), bf16[4,2,65536]{2,1,0:T(2,128)(2,1)S(1)}, u32[]{:S(2)}, u32[]{:S(2)}) async-start(bf16[4,2,65536]{2,1,0:T(2,128)(2,1)} %reshape.317), calls=%async_computation.1 | async-start | bytes 2097152 | tf_op jit(solution)/shard_map/all_to_all | solution.py:164
  726.9 360.6 %reduce-scatter.3.cloned.1.call-start = ((), (), s32[]{:S(2)}) async-start(), calls=%async_computation.4 | async-start | bytes 18874368 | tf_op jit(solution)/shard_map/reduce_scatter | solution.py:126
  737.8 0.6 copy-start.30
  737.8 0.7 copy-start.32
  737.8 0.7 copy-start.34
  737.9 402.9 %all-reduce.50.cloned.1.call-start = ((), (), s32[]{:S(2)}) async-start(), calls=%async_computation.7 | async-start | bytes 2228224 | tf_op jit(solution)/shard_map/psum | solution.py:192
  738.7 28.2 %copy-start.19 = (f32[64]{0:T(128)S(1)}, f32[64]{0:T(128)}, u32[]{:S(2)}) copy-start(f32[64]{0:T(128)} %copy-done.18) | copy-start | bytes 772
  738.7 28.2 %copy-start.21 = (f32[64]{0:T(128)S(1)}, f32[64]{0:T(128)}, u32[]{:S(2)}) copy-start(f32[64]{0:T(128)} %param.18) | copy-start | bytes 772
  738.7 28.2 %copy-start.23 = (f32[64]{0:T(128)S(1)}, f32[64]{0:T(128)}, u32[]{:S(2)}) copy-start(f32[64]{0:T(128)} %copy-done.22) | copy-start | bytes 772
  738.7 28.2 %copy-start.25 = (f32[64]{0:T(128)S(1)}, f32[64]{0:T(128)}, u32[]{:S(2)}) copy-start(f32[64]{0:T(128)} %param.19) | copy-start | bytes 772
  767.0 22.5 %copy-start.11 = (f32[8,64,4,16,16]{1,0,4,3,2:T(8,128)}, f32[8,64,4,16,16]{1,0,4,3,2:T(8,128)S(1)}, u32[]{:S(2)}) copy-start(f32[8,64,4,16,16]{1,0,4,3,2:T(8,128)S(1)} %copy.62) | copy-start | bytes 6291460
  767.0 32.6 %copy-start.28 = (f32[64]{0:T(128)S(1)}, f32[64]{0:T(128)}, u32[]{:S(2)}) copy-start(f32[64]{0:T(128)} %get-tuple-element.450) | copy-start | bytes 772
  1086.7 0.7 copy-start.15
  1086.7 114.5 %copy-start.1 = (bf16[128,4]{0,1:T(4,128)(2,1)S(1)}, bf16[128,4]{0,1:T(4,128)(2,1)}, u32[]{:S(2)}) copy-start(bf16[128,4]{0,1:T(4,128)(2,1)} %param.22) | copy-start | bytes 3076
  1087.5 98.4 %reduce-scatter.5.cloned.1.call-start = ((), (), s32[]{:S(2)}) async-start(), calls=%async_computation.5 | async-start | bytes 2621440 | tf_op jit(solution)/shard_map/reduce_scatter | solution.py:134
  1088.0 109.4 %all-reduce.48.cloned.1.call-start = ((), (), s32[]{:S(2)}) async-start(), calls=%async_computation.6 | async-start | bytes 2228224 | tf_op jit(solution)/shard_map/psum | solution.py:191
Sparse Core Ops, SparseCore 0:
  738.0 117.5 reduce-scatter.2
  1140.9 56.4 all-reduce.47
Sparse Core Ops, SparseCore 1:
  1087.5 53.2 all-reduce.49
  1142.9 42.9 reduce-scatter.4
